TPU v7x, 32 devices: a whole 2x2x4 slice. The times are simulated.
32 devices in a mesh: parts: 2 (over y), tiles: 8 (over z, x), mesh: 2 (over core).
Axes of the slice: x: 2, y: 2, z: 4, core: 2. Of those that a mesh axis runs over, the one named last changes fastest.
Arguments:
- patches: bfloat16 [1024, 128, 128], P(('parts', 'tiles', 'mesh')), parts along dimension 0, may hold values from -6 to 6
- send_index: int32 [32, 32], P(('parts', 'tiles', 'mesh')), parts along dimension 0, may hold values from 0 to 32, as said below
- pair_slots: int32 [32, 2, 16], P(('parts', 'tiles', 'mesh')), parts along dimension 0, may hold values from 0 to 32, as said below
- node_links: int32 [32, 4, 128], P(('parts', 'tiles', 'mesh')), parts along dimension 0, may hold values from 0 to 31
Outputs:
- pair_flow: float32 [2, 512], P(None, ('parts', 'tiles', 'mesh')), parts along dimension 1
- relaxed: float32 [2, 4096], P(None, ('parts', 'tiles', 'mesh')), parts along dimension 1
There are 2 independent parts, one for each index of `parts`. A program takes and returns all parts, laid end to end along the dimension named above; each array names one. Nothing has to cross between parts.
Inputs may be any that keep to these rules, and one draw needn't show every extreme that they name: `send_index`: each patch is sent to at most one owner, as one side of one tile pair; a live pair's two sides come from two different tiles and pair_slots names their received slots, numbered source tile times 4 plus slot; the value 2 * 16 marks an empty send slot. Some device fills all 4 slots to one peer. `pair_slots`: the value 8 * 4 marks a pair slot without a live pair; the number of live pairs differs from owner to owner, and some owner has all 16 slots live.
All inputs are finite; a program needn't handle non-finite values.
Results may differ from a plain program's by a relative error of at most 0.011.
Values may be sent and summed in bfloat16 or wider, within the bound.
No kernel may reach another device: no remote copies, remote signals or barrier semaphores. Data moves between devices by JAX's collectives and lax.ppermute only.
A program may use at most 64 MiB of HBM per device.

v0:
```python
import math
import jax
import jax.numpy as jnp
from jax import lax
from jax.sharding import PartitionSpec as P


def make_tables(side_len):
    ticks = jnp.arange(side_len, dtype=jnp.int32)
    product = ticks[:, None] * ticks[None, :] % side_len
    angle = 2.0 * math.pi / side_len * product.astype(jnp.float32)
    cosine = jnp.cos(angle) / math.sqrt(side_len)
    sine = jnp.sin(angle) / math.sqrt(side_len)
    coord = ticks.astype(jnp.float32)
    gap = coord[:, None] - coord[None, :]
    narrow = jnp.exp(-gap * gap / (2.0 * 0.35 * 0.35)) / (0.35 * math.sqrt(2.0 * math.pi))
    broad = jnp.exp(-gap * gap / 32.0) / (4.0 * math.sqrt(2.0 * math.pi))
    band = narrow - broad
    lag = jnp.where(coord < side_len / 2, coord, coord - side_len)
    return (cosine.astype(jnp.bfloat16), sine.astype(jnp.bfloat16), band.astype(jnp.bfloat16), lag)


def band_pass(stack, band):
    partial_value = jnp.einsum(
        "ij,bjk->bik", band, stack, preferred_element_type=jnp.float32
    ).astype(jnp.bfloat16)
    return jnp.einsum(
        "bij,kj->bik", partial_value, band, preferred_element_type=jnp.float32
    ).astype(jnp.bfloat16)


def prepare(stack, tables):
    cosine, sine, band, lag = tables
    filtered = band_pass(stack, band)
    left = jnp.concatenate([cosine, sine], 0)
    return jnp.einsum("ij,bjk->bik", left, filtered, preferred_element_type=jnp.float32).astype(
        jnp.bfloat16
    )


def finish(halves, tables):
    cosine, sine, band, lag = tables
    side_len = halves.shape[-1]
    count = halves.shape[0] // 2
    right = jnp.concatenate([cosine, sine], 1)
    back_left = jnp.concatenate([cosine, -sine], 1)
    quarter = jnp.einsum("bij,jk->bik", halves, right, preferred_element_type=jnp.float32)
    real_part = quarter[:, :side_len, :side_len] - quarter[:, side_len:, side_len:]
    imag_part = -(quarter[:, :side_len, side_len:] + quarter[:, side_len:, :side_len])
    moving_real, fixed_real = (real_part[:count], real_part[count:])
    moving_imag, fixed_imag = (imag_part[:count], imag_part[count:])
    power_real = moving_real * fixed_real + moving_imag * fixed_imag
    power_imag = moving_imag * fixed_real - moving_real * fixed_imag
    power = jnp.concatenate([power_real, power_imag], 1).astype(jnp.bfloat16)
    mixed = jnp.einsum("bij,jk->bik", power, right, preferred_element_type=jnp.float32)
    first = mixed[:, :side_len, :side_len] - mixed[:, side_len:, side_len:]
    second = mixed[:, :side_len, side_len:] + mixed[:, side_len:, :side_len]
    stacked = jnp.concatenate([first, second], 1).astype(jnp.bfloat16)
    surface = jnp.einsum("ij,bjk->bik", back_left, stacked, preferred_element_type=jnp.float32)
    weight = surface * surface
    denom = jnp.mean(weight, axis=(1, 2)) + 1e-06
    flow_y = jnp.mean(lag[None, :, None] * weight, axis=(1, 2)) / denom
    flow_x = jnp.mean(lag[None, None, :] * weight, axis=(1, 2)) / denom
    return jnp.stack([flow_y, flow_x], 0)


def per_device(patches, send_index, pair_slots, node_links):
    side_len = patches.shape[-1]
    patch_count = patches.shape[0]
    pair_count = pair_slots.shape[-1]
    tile_count = lax.axis_size("tiles")
    tables = make_tables(side_len)
    wanted = send_index[0]
    capacity = wanted.shape[0] // tile_count
    present = wanted < patch_count
    safe_wanted = jnp.minimum(wanted, patch_count - 1)
    picked = patches[safe_wanted]
    picked = jnp.where(present[:, None, None], picked, jnp.zeros_like(picked))
    received = lax.all_to_all(
        picked.reshape((tile_count, capacity) + patches.shape[1:]),
        "tiles",
        split_axis=0,
        concat_axis=0,
        tiled=True,
    )
    slot_total = tile_count * capacity
    received = received.reshape((slot_total,) + received.shape[2:])
    slots = pair_slots[0].reshape(-1)
    valid = slots < slot_total
    chosen = received[jnp.minimum(slots, slot_total - 1)]
    chosen = jnp.where(valid[:, None, None], chosen, jnp.zeros_like(chosen))
    block = min(16, pair_count)
    moving = chosen[:pair_count].reshape((pair_count // block, block) + chosen.shape[1:])
    fixed = chosen[pair_count:].reshape((pair_count // block, block) + chosen.shape[1:])

    def per_block(item):
        moving_part, fixed_part = item
        both = jnp.concatenate([moving_part, fixed_part], 0)
        both = prepare(both, tables)
        return finish(both, tables)

    flows = lax.map(per_block, (moving, fixed))
    pair_flow = jnp.transpose(flows, (1, 0, 2)).reshape(2, pair_count)
    flow_rows = lax.all_gather(pair_flow, "mesh", axis=1, tiled=True)
    linked = flow_rows[:, node_links[0]]
    relaxed = 0.5 * linked[:, 0] + 0.5 * jnp.mean(linked[:, 1:], axis=1)
    return (pair_flow, relaxed)


def solution(mesh):
    placed = (
        P(("parts", "tiles", "mesh"), None, None),
        P(("parts", "tiles", "mesh"), None),
        P(("parts", "tiles", "mesh"), None, None),
        P(("parts", "tiles", "mesh"), None, None),
    )
    return jax.shard_map(
        per_device,
        mesh=mesh,
        in_specs=placed,
        out_specs=(P(None, ("parts", "tiles", "mesh")), P(None, ("parts", "tiles", "mesh"))),
        check_vma=False,
    )
```

profile of v0, /device:TPU:0, one launch (start us, length us, event | category | flops | bytes accessed | tf_op | source)
XLA Modules:
  0.0 55.6 jit_solution(8383764545167968574)
XLA Ops:
  0.6 0.0 copy-start
  0.6 0.7 %fusion.57 = s32[32]{0:T(128)S(1)} fusion(s32[1,32]{1,0:T(1,128)} %param.5), kind=kLoop, calls=%fused_computation.76 | loop fusion | flops 128 | bytes 256 | tf_op jit(solution)/shard_map/select_n | solution.py:77
  1.4 0.7 %compare_reduce_fusion = pred[32]{0:T(512)(128)(4,1)S(1)} fusion(s32[1,32]{1,0:T(1,128)} %param.5), kind=kLoop, calls=%fused_computation.71 | loop fusion | flops 32 | bytes 160 | tf_op jit(solution)/shard_map/lt | solution.py:75
  2.1 0.1 lt.91
  2.2 0.0 copy-done
  2.2 0.8 %gather_fusion = bf16[32,128,128]{2,1,0:T(8,128)(2,1)S(1)} fusion(bf16[32,128,128]{2,1,0:T(8,128)(2,1)S(1)} %copy-done, s32[1024]{0:T(1024)S(1)} %pad_clamp_fusion.2), kind=kCustom, calls=%fused_computation | custom fusion | bytes 2097280 | tf_op jit(solution)/shard_map/gather | solution.py:77
  2.9 0.0 copy-start.2
  2.9 0.0 copy-start.1
  2.9 1.1 %broadcast_select_fusion = bf16[8,4,128,128]{3,2,1,0:T(8,128)(2,1)} fusion(bf16[8,4,128,128]{3,2,1,0:T(8,128)(2,1)S(1)} %bitcast.55, pred[8,4]{1,0:T(8,128)(4,1)S(1)} %lt.91), kind=kLoop, calls=%fused_computation.31 | loop fusion | flops 524288 | bytes 2097184 | tf_op jit(solution)/shard_map/jit(_where)/select_n | solution.py:78
  4.1 7.3 %all-to-all-start = ((bf16[8,4,128,128]{3,2,1,0:T(8,128)(2,1)}), bf16[8,4,128,128]{3,2,1,0:T(8,128)(2,1)S(1)}, u32[]{:S(2)}, u32[]{:S(2)}) async-start(bf16[8,4,128,128]{3,2,1,0:T(8,128)(2,1)} %broadcast_select_fusion), calls=%async_computation | async-start | bytes 2097152 | tf_op jit(solution)/shard_map/all_to_all | solution.py:79
  11.4 0.0 copy-done.2
  11.4 0.1 min.29
  11.5 0.1 lt.89
  11.6 0.0 copy-done.1
  11.6 0.3 fusion.53
  11.9 0.3 multiply_convert_fusion
  12.2 25.0 %all-to-all-done = bf16[8,4,128,128]{3,2,1,0:T(8,128)(2,1)S(1)} async-done(((bf16[8,4,128,128]{3,2,1,0:T(8,128)(2,1)}), bf16[8,4,128,128]{3,2,1,0:T(8,128)(2,1)S(1)}, u32[]{:S(2)}, u32[]{:S(2)}) %all-to-all-start) | async-done | bytes 1048608 | tf_op jit(solution)/shard_map/all_to_all | solution.py:79
  37.1 0.7 %gather_fusion.1 = bf16[32,128,128]{2,1,0:T(8,128)(2,1)S(1)} fusion(bf16[32,128,128]{2,1,0:T(8,128)(2,1)S(1)} %bitcast.54, s32[1024]{0:T(1024)S(1)} %pad_clamp_fusion.1), kind=kCustom, calls=%fused_computation.1 | custom fusion | bytes 2097280 | tf_op jit(solution)/shard_map/gather | solution.py:90
  37.9 1.3 %convolution_convert_fusion = bf16[32,128,128]{2,1,0:T(8,128)(2,1)S(1)} fusion(bf16[32,128,128]{2,1,0:T(8,128)(2,1)S(1)} %gather_fusion.1, pred[32]{0:T(512)(128)(4,1)S(1)} %lt.89, f32[128]{0:T(128)S(1)} %iota_convert_fusion), kind=kOutput, calls=%fused_computation.11 | convolution fusion | flops 270303232 | bytes 2097696 | tf_op jit(solution)/shard_map/while/body/eval_jaxpr/bij,kj->bik/dot_general | solution.py:27
  39.2 5.8 %fusion.1 = f32[32,256,256]{2,1,0:T(8,128)} fusion(bf16[32,128,128]{2,1,0:T(8,128)(2,1)S(1)} %convolution_convert_fusion, bf16[128,128]{1,0:T(8,128)(2,1)S(1)} %get-tuple-element.37, bf16[128,128]{1,0:T(8,128)(2,1)S(1)} %get-tuple-element.38), kind=kOutput, calls=%fused_computation.6 | convolution fusion | flops 806617088 | bytes 9502720 | tf_op jit(solution)/shard_map/while/body/eval_jaxpr/bij,jk->bik/dot_general | solution.py:47
  45.0 4.4 %slice_subtract_fusion = (f32[32,128,128]{2,1,0:T(8,128)S(1)}, f32[32,128,128]{2,1,0:T(8,128)S(1)}) fusion(f32[32,256,256]{2,1,0:T(8,128)} %fusion.1), kind=kLoop, calls=%fused_computation.5 | loop fusion | flops 1572864 | bytes 12582912 | tf_op jit(solution)/shard_map/while/body/eval_jaxpr/sub | solution.py:48
  49.3 0.4 add_convert_fusion
  49.7 0.7 %fusion.9 = f32[16,256,256]{2,1,0:T(8,128)S(1)} fusion(bf16[16,128,128]{2,1,0:T(8,128)(2,1)S(1)} %get-tuple-element.34, bf16[16,128,128]{2,1,0:T(8,128)(2,1)S(1)} %get-tuple-element.33, bf16[128,128]{1,0:T(8,128)(2,1)S(1)} %get-tuple-element.38, bf16[128,128]{1,0:T(8,128)(2,1)S(1)} %get-tuple-element.37), kind=kOutput, calls=%fused_computation.18 | convolution fusion | flops 270663680 | bytes 5308416 | tf_op jit(solution)/shard_map/while/body/eval_jaxpr/bij,jk->bik/dot_general | solution.py:55
  50.4 0.3 fusion.8
  50.7 0.6 %multiply_reduce_fusion.1 = (f32[16]{0:T(128)S(1)}, f32[16]{0:T(128)S(1)}, f32[16]{0:T(128)S(1)}) fusion(f32[128]{0:T(128)S(1)} %compare_select_fusion.3, bf16[128,128]{1,0:T(8,128)(2,1)S(1)} %get-tuple-element.38, bf16[128,128]{1,0:T(8,128)(2,1)S(1)} %fusion.53, bf16[16,128,128]{2,1,0:T(8,128)(2,1)S(1)} %get-tuple-element.32, ...), kind=kOutput, calls=%fused_computation.26 | convolution fusion | flops 138018768 | bytes 1114816 | tf_op jit(solution)/shard_map/while/body/eval_jaxpr/ij,bjk->bik/dot_general | solution.py:59
  51.4 0.6 %pad_maximum_fusion.2 = f32[2,16]{1,0:T(2,128)} fusion(f32[1,16]{1,0:T(1,128)S(1)} %get-tuple-element.36, f32[1,16]{1,0:T(1,128)S(1)} %get-tuple-element.35), kind=kLoop, calls=%fused_computation.75 | loop fusion | flops 32 | bytes 256 | tf_op jit(solution)/shard_map/while/body/eval_jaxpr/stack | solution.py:64
  51.9 1.8 %all-gather = f32[2,16,2]{1,2,0:T(2,128)S(1)} all-gather(f32[1,16,2]{1,2,0:T(2,128)S(1)} %fusion.76), channel_id=1, replica_groups=mesh['parts'=2,'tiles'=8,'mesh'=2] {'mesh'}, dimensions={0}, use_global_device_ids=true | all-gather | bytes 384 | tf_op jit(solution)/shard_map/all_gather | solution.py:104
  53.7 0.1 copy.34
  53.8 1.0 %gather_fusion.2 = f32[512,2]{1,0:T(8,128)S(1)} fusion(f32[2,32]{0,1:T(8,128)S(1)} %bitcast.57, s32[1024]{0:T(1024)S(1)} %pad_clamp_fusion), kind=kCustom, calls=%fused_computation.2 | custom fusion | bytes 10240 | tf_op jit(solution)/shard_map/gather | solution.py:105
  54.9 0.1 copy.28
  55.0 0.6 %fusion.56 = f32[2,128]{1,0:T(2,128)} fusion(f32[2,4,128]{2,0,1:T(2,128)S(1)} %bitcast.59, f32[2,128]{1,0:T(2,128)S(1)} %slice_reduce_fusion), kind=kLoop, calls=%fused_computation.74 | loop fusion | flops 768 | bytes 3072 | tf_op jit(solution)/shard_map/add | solution.py:106
  (12 shorter events, 0.1 us)
Async XLA Ops:
  0.6 1.5 %copy-start = (bf16[32,128,128]{2,1,0:T(8,128)(2,1)S(1)}, bf16[32,128,128]{2,1,0:T(8,128)(2,1)}, u32[]{:S(2)}) copy-start(bf16[32,128,128]{2,1,0:T(8,128)(2,1)} %param.4) | copy-start | bytes 3145732
  2.9 8.4 %copy-start.2 = (s32[1,2,16]{2,1,0:T(2,128)S(1)}, s32[1,2,16]{2,1,0:T(2,128)}, u32[]{:S(2)}) copy-start(s32[1,2,16]{2,1,0:T(2,128)} %param.6) | copy-start | bytes 388
  2.9 8.6 %copy-start.1 = (s32[1,4,128]{2,1,0:T(4,128)S(1)}, s32[1,4,128]{2,1,0:T(4,128)}, u32[]{:S(2)}) copy-start(s32[1,4,128]{2,1,0:T(4,128)} %param.7) | copy-start | bytes 6148
  4.1 33.0 %all-to-all-start = ((bf16[8,4,128,128]{3,2,1,0:T(8,128)(2,1)}), bf16[8,4,128,128]{3,2,1,0:T(8,128)(2,1)S(1)}, u32[]{:S(2)}, u32[]{:S(2)}) async-start(bf16[8,4,128,128]{3,2,1,0:T(8,128)(2,1)} %broadcast_select_fusion), calls=%async_computation | async-start | bytes 2097152 | tf_op jit(solution)/shard_map/all_to_all | solution.py:79
where the time goes:
time: 55.8 us; the launch traced here: 55.6 us
  waiting for transfers between devices  25 us (45%)
  other arithmetic  9.36 us (17%)
  matrix products  8.41 us (15%)
  starting transfers between devices  7.28 us (13%)
  local copies, waits for them, and re-layouts  3 us (5%)
  blocking collectives  1.79 us (3%)
  between operations  0.78 us (1%)
    all_to_all x1, waiting for transfers between devices, per_device(): lax.all_to_all(picked.reshape((tile_count, capacity) + patches.shape[1:])...  25 us
    all_to_all x1, starting transfers between devices, per_device(): lax.all_to_all(picked.reshape((tile_count, capacity) + patches.shape[1:])...  7.28 us
    dot_general x1, matrix products, finish(): jnp.einsum('bij,jk->bik', halves, right, preferred_element_type=jnp.float32)  5.76 us
    sub x1, other arithmetic, finish(): quarter[:, :side_len, :side_len] - quarter[:, side_len:, side_len:]  4.35 us
    all_gather x1, blocking collectives, per_device(): flow_rows = lax.all_gather(pair_flow, 'mesh', axis=1, tiled=True)  1.79 us
    dot_general x1, matrix products, band_pass(): jnp.einsum('bij,kj->bik', partial_value, band, preferred_element_type=jnp...  1.31 us
    gather x2, local copies, waits for them, and re-layouts, per_device(): linked = flow_rows[:, node_links[0]]  1.14 us
    select_n x1, other arithmetic, per_device(): picked = jnp.where(present[:, None, None], picked, jnp.zeros_like(picked))  1.13 us
  transfers between devices with their start and end apart: 1, of which 1 were waited for; matrix products, arithmetic and copies ran while one was open for 1% of the time, Pallas kernels for 0%

commit v1 on v0

--- a/solution.py
+++ b/solution.py
@@ -3,6 +3,18 @@
 import jax.numpy as jnp
 from jax import lax
 from jax.sharding import PartitionSpec as P
+
+
+def sent_to_each(x, axis, split, join):
+    ways, here = (lax.axis_size(axis), lax.axis_index(axis))
+    width = x.shape[split] // ways
+    turned = jnp.roll(x, -here * width, axis=split)
+    got = [lax.slice_in_dim(turned, 0, width, axis=split)]
+    for far in range(1, ways):
+        sent = lax.slice_in_dim(turned, far * width, (far + 1) * width, axis=split)
+        got.append(lax.ppermute(sent, axis, [(d, (d + far) % ways) for d in range(ways)]))
+    line = jnp.concatenate(got[::-1], axis=join)
+    return jnp.roll(line, (here + 1) * got[0].shape[join], axis=join)
 
 
 def make_tables(side_len):
@@ -76,12 +88,8 @@
     safe_wanted = jnp.minimum(wanted, patch_count - 1)
     picked = patches[safe_wanted]
     picked = jnp.where(present[:, None, None], picked, jnp.zeros_like(picked))
-    received = lax.all_to_all(
-        picked.reshape((tile_count, capacity) + patches.shape[1:]),
-        "tiles",
-        split_axis=0,
-        concat_axis=0,
-        tiled=True,
+    received = sent_to_each(
+        picked.reshape((tile_count, capacity) + patches.shape[1:]), "tiles", 0, 0
     )
     slot_total = tile_count * capacity
     received = received.reshape((slot_total,) + received.shape[2:])

time: 55.8 us -> 53.5 us (0.959)
  waiting for transfers between devices: 25 us -> 14.8 us
  starting transfers between devices: 7.28 us -> 12.5 us
  local copies, waits for them, and re-layouts: 3 us -> 5.04 us
    all_to_all x1 -> x0, waiting for transfers between devices: 25 us -> none  [per_device(): lax.all_to_all(picked.reshape((tile_count, capacity) + patches.shape[1:])...]
    ppermute x0 -> x7, waiting for transfers between devices: none -> 14.8 us  [sent_to_each(): lax.ppermute(sent, axis, [(d, (d + far) % ways) for d in range(ways)])]
    ppermute x0 -> x7, starting transfers between devices: none -> 12.5 us  [sent_to_each(): lax.ppermute(sent, axis, [(d, (d + far) % ways) for d in range(ways)])]
    all_to_all x1 -> x0, starting transfers between devices: 7.28 us -> none  [per_device(): lax.all_to_all(picked.reshape((tile_count, capacity) + patches.shape[1:])...]
    unnamed x7 -> x14, local copies, waits for them, and re-layouts: 0.11 us -> 2.04 us
    select_n x1, other arithmetic: 1.13 us -> 0.14 us  [per_device(): picked = jnp.where(present[:, None, None], picked, jnp.zeros_like(picked))]
    concatenate x0 -> x2, other arithmetic: none -> 0.79 us  [the longest x1 0.39 us: sent_to_each(): turned = jnp.roll(x, -here * width, axis=split)]
    min x1, other arithmetic: 0.01 us -> 0.77 us  [per_device(): chosen = received[jnp.minimum(slots, slot_total - 1)]]
  transfers between devices with their start and end apart: 1 -> 7, of which waited for: 1 -> 3; matrix products, arithmetic and copies ran while one was open for 1% -> 5% of each run, Pallas kernels for 0% -> 0%
where the time goes in v1:
time: 53.5 us; the launch traced here: 53.3 us
  waiting for transfers between devices  14.8 us (28%)
  starting transfers between devices  12.5 us (23%)
  other arithmetic  9.82 us (18%)
  matrix products  8.39 us (16%)
  local copies, waits for them, and re-layouts  5.04 us (9%)
  blocking collectives  1.79 us (3%)
  between operations  0.92 us (2%)
    ppermute x7, waiting for transfers between devices, sent_to_each(): lax.ppermute(sent, axis, [(d, (d + far) % ways) for d in range(ways)])  14.8 us
    ppermute x7, starting transfers between devices, sent_to_each(): lax.ppermute(sent, axis, [(d, (d + far) % ways) for d in range(ways)])  12.5 us
    dot_general x1, matrix products, finish(): jnp.einsum('bij,jk->bik', halves, right, preferred_element_type=jnp.float32)  5.76 us
    sub x1, other arithmetic, finish(): quarter[:, :side_len, :side_len] - quarter[:, side_len:, side_len:]  4.35 us
    unnamed x14, local copies, waits for them, and re-layouts  2.04 us
    all_gather x1, blocking collectives, per_device(): flow_rows = lax.all_gather(pair_flow, 'mesh', axis=1, tiled=True)  1.79 us
    dot_general x1, matrix products, band_pass(): jnp.einsum('bij,kj->bik', partial_value, band, preferred_element_type=jnp...  1.3 us
    gather x2, local copies, waits for them, and re-layouts, per_device(): linked = flow_rows[:, node_links[0]]  1.14 us
  transfers between devices with their start and end apart: 7, of which 3 were waited for; matrix products, arithmetic and copies ran while one was open for 5% of the time, Pallas kernels for 0%

profile of v1, /device:TPU:0, one launch (start us, length us, event | category | flops | bytes accessed | tf_op | source)
XLA Modules:
  0.0 53.3 jit_solution(9475157627385634729)
XLA Ops:
  0.6 0.0 copy-start
  0.7 0.8 %broadcast_minimum_fusion = s32[1,2,16]{2,1,0:T(2,128)S(1)} fusion(s32[1,2,16]{2,1,0:T(2,128)} %param.8), kind=kLoop, calls=%fused_computation.95 | loop fusion | flops 32 | bytes 256 | tf_op jit(solution)/shard_map/min | solution.py:98
  1.4 0.1 min.29
  1.5 0.7 %compare_reduce_fusion = pred[32]{0:T(512)(128)(4,1)S(1)} fusion(s32[1,32]{1,0:T(1,128)} %param.7), kind=kLoop, calls=%fused_computation.85 | loop fusion | flops 32 | bytes 160 | tf_op jit(solution)/shard_map/lt | solution.py:87
  2.2 0.7 %fusion.59 = (s32[32]{0:T(128)S(1)}, s32[32]{0:T(128)S(1)}) fusion(s32[1,32]{1,0:T(1,128)} %param.7, s32[32,1]{0,1:T(1,128)S(1)} %min.29), kind=kLoop, calls=%fused_computation.90 | loop fusion | flops 224 | bytes 512 | tf_op jit(solution)/shard_map/select_n | solution.py:89
  2.9 0.1 lt.100
  2.9 0.0 copy-done
  3.0 0.8 %gather_fusion = bf16[32,128,128]{2,1,0:T(8,128)(2,1)S(1)} fusion(bf16[32,128,128]{2,1,0:T(8,128)(2,1)S(1)} %copy-done, s32[1024]{0:T(1024)S(1)} %pad_clamp_fusion.2), kind=kCustom, calls=%fused_computation | custom fusion | bytes 2097280 | tf_op jit(solution)/shard_map/gather | solution.py:89
  3.7 0.1 broadcast_select_fusion
  3.9 0.0 copy-start.2
  3.9 0.0 copy-start.1
  3.9 0.4 fusion.8
  4.3 0.1 fusion.77
  4.4 6.1 %collective-permute-start = (bf16[1,4,128,128]{3,2,1,0:T(8,128)(2,1)S(1)}, bf16[1,4,128,128]{3,2,1,0:T(8,128)(2,1)}, u32[]{:S(2)}, u32[]{:S(2)}) collective-permute-start(bf16[1,4,128,128]{3,2,1,0:T(8,128)(2,1)S(1)} %get-tuple-element.42), channel_id=1, source_target_pairs={{0,14},{2,0},{4,2},{6,4},{8,6},{10,8},{12,10},{14,12},{1,15},{3,1}... | collective-permute-start | bytes 393224 | tf_op jit(solution)/shard_map/ppermute | solution.py:15
  10.4 0.4 collective-permute-start.1
  10.9 0.0 collective-permute-start.2
  10.9 3.0 %collective-permute-start.3 = (bf16[1,4,128,128]{3,2,1,0:T(8,128)(2,1)S(1)}, bf16[1,4,128,128]{3,2,1,0:T(8,128)(2,1)S(1)}, u32[]{:S(2)}, u32[]{:S(2)}) collective-permute-start(bf16[1,4,128,128]{3,2,1,0:T(8,128)(2,1)S(1)} %get-tuple-element.39), channel_id=1, source_target_pairs={{0,8},{2,10},{4,12},{6,14},{8,0},{10,2},{12,4},{14,6},{1,9},{3,11}... | collective-permute-start | bytes 393224 | tf_op jit(solution)/shard_map/ppermute | solution.py:15
  13.9 0.0 collective-permute-start.4
  13.9 0.0 copy-done.2
  13.9 0.3 multiply_convert_fusion
  14.2 0.3 fusion.55
  14.6 0.1 lt.98
  14.6 0.0 collective-permute-done
  14.6 1.8 %collective-permute-start.5 = (bf16[1,4,128,128]{3,2,1,0:T(8,128)(2,1)S(1)}, bf16[1,4,128,128]{3,2,1,0:T(8,128)(2,1)S(1)}, u32[]{:S(2)}, u32[]{:S(2)}) collective-permute-start(bf16[1,4,128,128]{3,2,1,0:T(8,128)(2,1)S(1)} %get-tuple-element.37), channel_id=1, source_target_pairs={{0,4},{2,6},{4,8},{6,10},{8,12},{10,14},{12,0},{14,2},{1,5},{3,7},... | collective-permute-start | bytes 393224 | tf_op jit(solution)/shard_map/ppermute | solution.py:15
  16.5 0.9 %constant_dynamic-update-slice_fusion.6 = bf16[8,4,128,128]{3,2,1,0:T(8,128)(2,1)S(1)} fusion(bf16[1,4,128,128]{3,2,1,0:T(8,128)(2,1)} %collective-permute-done), kind=kLoop, calls=%fused_computation.74 | loop fusion | bytes 262144
  17.4 0.0 collective-permute-done.1
  17.4 1.2 %collective-permute-start.6 = (bf16[1,4,128,128]{3,2,1,0:T(8,128)(2,1)S(1)}, bf16[1,4,128,128]{3,2,1,0:T(8,128)(2,1)S(1)}, u32[]{:S(2)}, u32[]{:S(2)}) collective-permute-start(bf16[1,4,128,128]{3,2,1,0:T(8,128)(2,1)S(1)} %get-tuple-element.36), channel_id=1, source_target_pairs={{0,2},{2,4},{4,6},{6,8},{8,10},{10,12},{12,14},{14,0},{1,3},{3,5},... | collective-permute-start | bytes 393224 | tf_op jit(solution)/shard_map/ppermute | solution.py:15
  18.6 0.9 %constant_dynamic-update-slice_fusion.5 = bf16[8,4,128,128]{3,2,1,0:T(8,128)(2,1)S(1)} fusion(bf16[8,4,128,128]{3,2,1,0:T(8,128)(2,1)S(1)} %constant_dynamic-update-slice_fusion.6, bf16[1,4,128,128]{3,2,1,0:T(8,128)(2,1)} %collective-permute-done.1), kind=kLoop, calls=%fused_computation.73 | loop fusion | bytes 262144
  19.5 0.5 collective-permute-done.2
  20.0 12.7 %collective-permute-done.3 = bf16[1,4,128,128]{3,2,1,0:T(8,128)(2,1)S(1)} collective-permute-done((bf16[1,4,128,128]{3,2,1,0:T(8,128)(2,1)S(1)}, bf16[1,4,128,128]{3,2,1,0:T(8,128)(2,1)S(1)}, u32[]{:S(2)}, u32[]{:S(2)}) %collective-permute-start.3) | collective-permute-done | bytes 131104 | tf_op jit(solution)/shard_map/ppermute | solution.py:15
  32.8 1.6 %collective-permute-done.4 = bf16[1,4,128,128]{3,2,1,0:T(8,128)(2,1)S(1)} collective-permute-done((bf16[1,4,128,128]{3,2,1,0:T(8,128)(2,1)S(1)}, bf16[1,4,128,128]{3,2,1,0:T(8,128)(2,1)S(1)}, u32[]{:S(2)}, u32[]{:S(2)}) %collective-permute-start.4) | collective-permute-done | bytes 131104 | tf_op jit(solution)/shard_map/ppermute | solution.py:15
  34.4 0.0 collective-permute-done.5
  34.4 0.0 collective-permute-done.6
  34.5 0.4 fusion.7
  34.9 0.7 %gather_fusion.1 = bf16[32,128,128]{2,1,0:T(8,128)(2,1)S(1)} fusion(bf16[32,128,128]{2,1,0:T(8,128)(2,1)S(1)} %bitcast.54, s32[1024]{0:T(1024)S(1)} %pad_clamp_fusion.1), kind=kCustom, calls=%fused_computation.1 | custom fusion | bytes 2097280 | tf_op jit(solution)/shard_map/gather | solution.py:98
  35.6 1.3 %convolution_convert_fusion = bf16[32,128,128]{2,1,0:T(8,128)(2,1)S(1)} fusion(bf16[32,128,128]{2,1,0:T(8,128)(2,1)S(1)} %gather_fusion.1, pred[32]{0:T(512)(128)(4,1)S(1)} %lt.98, f32[128]{0:T(128)S(1)} %iota_convert_fusion), kind=kOutput, calls=%fused_computation.15 | convolution fusion | flops 270303232 | bytes 2097696 | tf_op jit(solution)/shard_map/while/body/eval_jaxpr/bij,kj->bik/dot_general | solution.py:39
  36.9 5.8 %fusion.1 = f32[32,256,256]{2,1,0:T(8,128)} fusion(bf16[32,128,128]{2,1,0:T(8,128)(2,1)S(1)} %convolution_convert_fusion, bf16[128,128]{1,0:T(8,128)(2,1)S(1)} %get-tuple-element.47, bf16[128,128]{1,0:T(8,128)(2,1)S(1)} %get-tuple-element.48), kind=kOutput, calls=%fused_computation.10 | convolution fusion | flops 806617088 | bytes 9502720 | tf_op jit(solution)/shard_map/while/body/eval_jaxpr/bij,jk->bik/dot_general | solution.py:59
  42.7 4.4 %slice_subtract_fusion = (f32[32,128,128]{2,1,0:T(8,128)S(1)}, f32[32,128,128]{2,1,0:T(8,128)S(1)}) fusion(f32[32,256,256]{2,1,0:T(8,128)} %fusion.1), kind=kLoop, calls=%fused_computation.5 | loop fusion | flops 1572864 | bytes 12582912 | tf_op jit(solution)/shard_map/while/body/eval_jaxpr/sub | solution.py:60
  47.0 0.4 add_convert_fusion
  47.4 0.7 %fusion.11 = f32[16,256,256]{2,1,0:T(8,128)S(1)} fusion(bf16[16,128,128]{2,1,0:T(8,128)(2,1)S(1)} %get-tuple-element.35, bf16[16,128,128]{2,1,0:T(8,128)(2,1)S(1)} %get-tuple-element.34, bf16[128,128]{1,0:T(8,128)(2,1)S(1)} %get-tuple-element.48, bf16[128,128]{1,0:T(8,128)(2,1)S(1)} %get-tuple-element.47), kind=kOutput, calls=%fused_computation.24 | convolution fusion | flops 270663680 | bytes 5308416 | tf_op jit(solution)/shard_map/while/body/eval_jaxpr/bij,jk->bik/dot_general | solution.py:67
  48.1 0.3 fusion.10
  48.4 0.6 %multiply_reduce_fusion.1 = (f32[16]{0:T(128)S(1)}, f32[16]{0:T(128)S(1)}, f32[16]{0:T(128)S(1)}) fusion(f32[128]{0:T(128)S(1)} %compare_select_fusion.3, bf16[128,128]{1,0:T(8,128)(2,1)S(1)} %get-tuple-element.48, bf16[128,128]{1,0:T(8,128)(2,1)S(1)} %fusion.55, bf16[16,128,128]{2,1,0:T(8,128)(2,1)S(1)} %get-tuple-element.33, ...), kind=kOutput, calls=%fused_computation.32 | convolution fusion | flops 138018768 | bytes 1114816 | tf_op jit(solution)/shard_map/while/body/eval_jaxpr/ij,bjk->bik/dot_general | solution.py:71
  49.1 0.6 %pad_maximum_fusion.2 = f32[2,16]{1,0:T(2,128)} fusion(f32[1,16]{1,0:T(1,128)S(1)} %get-tuple-element.44, f32[1,16]{1,0:T(1,128)S(1)} %get-tuple-element.43), kind=kLoop, calls=%fused_computation.89 | loop fusion | flops 32 | bytes 256 | tf_op jit(solution)/shard_map/while/body/eval_jaxpr/stack | solution.py:76
  49.7 1.8 %all-gather = f32[2,16,2]{1,2,0:T(2,128)S(1)} all-gather(f32[1,16,2]{1,2,0:T(2,128)S(1)} %fusion.79), channel_id=1, replica_groups=mesh['parts'=2,'tiles'=8,'mesh'=2] {'mesh'}, dimensions={0}, use_global_device_ids=true | all-gather | bytes 384 | tf_op jit(solution)/shard_map/all_gather | solution.py:112
  51.5 0.1 copy.34
  51.5 1.0 %gather_fusion.2 = f32[512,2]{1,0:T(8,128)S(1)} fusion(f32[2,32]{0,1:T(8,128)S(1)} %bitcast.57, s32[1024]{0:T(1024)S(1)} %pad_clamp_fusion), kind=kCustom, calls=%fused_computation.2 | custom fusion | bytes 10240 | tf_op jit(solution)/shard_map/gather | solution.py:113
  52.6 0.1 copy.28
  52.7 0.6 %fusion.58 = f32[2,128]{1,0:T(2,128)} fusion(f32[2,4,128]{2,0,1:T(2,128)S(1)} %bitcast.59, f32[2,128]{1,0:T(2,128)S(1)} %slice_reduce_fusion), kind=kLoop, calls=%fused_computation.88 | loop fusion | flops 768 | bytes 3072 | tf_op jit(solution)/shard_map/add | solution.py:114
  (17 shorter events, 0.2 us)
Async XLA Ops:
  0.6 2.3 %copy-start = (bf16[32,128,128]{2,1,0:T(8,128)(2,1)S(1)}, bf16[32,128,128]{2,1,0:T(8,128)(2,1)}, u32[]{:S(2)}) copy-start(bf16[32,128,128]{2,1,0:T(8,128)(2,1)} %param.6) | copy-start | bytes 3145732
  3.9 10.0 %copy-start.2 = (s32[1,2,16]{2,1,0:T(2,128)S(1)}, s32[1,2,16]{2,1,0:T(2,128)}, u32[]{:S(2)}) copy-start(s32[1,2,16]{2,1,0:T(2,128)} %param.8) | copy-start | bytes 388
  3.9 10.6 %copy-start.1 = (s32[1,4,128]{2,1,0:T(4,128)S(1)}, s32[1,4,128]{2,1,0:T(4,128)}, u32[]{:S(2)}) copy-start(s32[1,4,128]{2,1,0:T(4,128)} %param.9) | copy-start | bytes 6148
  4.4 10.3 %collective-permute-start = (bf16[1,4,128,128]{3,2,1,0:T(8,128)(2,1)S(1)}, bf16[1,4,128,128]{3,2,1,0:T(8,128)(2,1)}, u32[]{:S(2)}, u32[]{:S(2)}) collective-permute-start(bf16[1,4,128,128]{3,2,1,0:T(8,128)(2,1)S(1)} %get-tuple-element.42), channel_id=1, source_target_pairs={{0,14},{2,0},{4,2},{6,4},{8,6},{10,8},{12,10},{14,12},{1,15},{3,1}... | collective-permute-start | bytes 393224 | tf_op jit(solution)/shard_map/ppermute | solution.py:15
  10.4 6.9 %collective-permute-start.1 = (bf16[1,4,128,128]{3,2,1,0:T(8,128)(2,1)S(1)}, bf16[1,4,128,128]{3,2,1,0:T(8,128)(2,1)}, u32[]{:S(2)}, u32[]{:S(2)}) collective-permute-start(bf16[1,4,128,128]{3,2,1,0:T(8,128)(2,1)S(1)} %get-tuple-element.41), channel_id=1, source_target_pairs={{0,12},{2,14},{4,0},{6,2},{8,4},{10,6},{12,8},{14,10},{1,13},{3,15... | collective-permute-start | bytes 393224 | tf_op jit(solution)/shard_map/ppermute | solution.py:15
  10.9 9.1 %collective-permute-start.2 = (bf16[1,4,128,128]{3,2,1,0:T(8,128)(2,1)S(1)}, bf16[1,4,128,128]{3,2,1,0:T(8,128)(2,1)S(1)}, u32[]{:S(2)}, u32[]{:S(2)}) collective-permute-start(bf16[1,4,128,128]{3,2,1,0:T(8,128)(2,1)S(1)} %get-tuple-element.40), channel_id=1, source_target_pairs={{0,10},{2,12},{4,14},{6,0},{8,2},{10,4},{12,6},{14,8},{1,11},{3,13... | collective-permute-start | bytes 393224 | tf_op jit(solution)/shard_map/ppermute | solution.py:15
  10.9 21.9 %collective-permute-start.3 = (bf16[1,4,128,128]{3,2,1,0:T(8,128)(2,1)S(1)}, bf16[1,4,128,128]{3,2,1,0:T(8,128)(2,1)S(1)}, u32[]{:S(2)}, u32[]{:S(2)}) collective-permute-start(bf16[1,4,128,128]{3,2,1,0:T(8,128)(2,1)S(1)} %get-tuple-element.39), channel_id=1, source_target_pairs={{0,8},{2,10},{4,12},{6,14},{8,0},{10,2},{12,4},{14,6},{1,9},{3,11}... | collective-permute-start | bytes 393224 | tf_op jit(solution)/shard_map/ppermute | solution.py:15
  13.9 20.4 %collective-permute-start.4 = (bf16[1,4,128,128]{3,2,1,0:T(8,128)(2,1)S(1)}, bf16[1,4,128,128]{3,2,1,0:T(8,128)(2,1)S(1)}, u32[]{:S(2)}, u32[]{:S(2)}) collective-permute-start(bf16[1,4,128,128]{3,2,1,0:T(8,128)(2,1)S(1)} %get-tuple-element.38), channel_id=1, source_target_pairs={{0,6},{2,8},{4,10},{6,12},{8,14},{10,0},{12,2},{14,4},{1,7},{3,9},... | collective-permute-start | bytes 393224 | tf_op jit(solution)/shard_map/ppermute | solution.py:15
  14.6 19.7 %collective-permute-start.5 = (bf16[1,4,128,128]{3,2,1,0:T(8,128)(2,1)S(1)}, bf16[1,4,128,128]{3,2,1,0:T(8,128)(2,1)S(1)}, u32[]{:S(2)}, u32[]{:S(2)}) collective-permute-start(bf16[1,4,128,128]{3,2,1,0:T(8,128)(2,1)S(1)} %get-tuple-element.37), channel_id=1, source_target_pairs={{0,4},{2,6},{4,8},{6,10},{8,12},{10,14},{12,0},{14,2},{1,5},{3,7},... | collective-permute-start | bytes 393224 | tf_op jit(solution)/shard_map/ppermute | solution.py:15
  17.4 17.0 %collective-permute-start.6 = (bf16[1,4,128,128]{3,2,1,0:T(8,128)(2,1)S(1)}, bf16[1,4,128,128]{3,2,1,0:T(8,128)(2,1)S(1)}, u32[]{:S(2)}, u32[]{:S(2)}) collective-permute-start(bf16[1,4,128,128]{3,2,1,0:T(8,128)(2,1)S(1)} %get-tuple-element.36), channel_id=1, source_target_pairs={{0,2},{2,4},{4,6},{6,8},{8,10},{10,12},{12,14},{14,0},{1,3},{3,5},... | collective-permute-start | bytes 393224 | tf_op jit(solution)/shard_map/ppermute | solution.py:15
